TPU v7x, 512 devices: a whole 4x8x8 slice. The times are simulated.
512 devices in a mesh: grp: 8 (over z_hi, core), shard: 64 (over z_lo, y, x).
Axes of the slice: x: 4, y: 8, z: 8 (z_hi: 4, z_lo: 2; z = z_hi * 2 + z_lo), core: 2. Of those that a mesh axis runs over, the one named last changes fastest.
Arguments:
- gradients: float32 [8, 1024, 512], P('grp', 'shard'), may hold values from -6 to 6
- weight: float32 [1024, 512], P('shard'), may hold values from -0.1875 to 0.1875
- moment: float32 [1024, 512], P('shard'), may hold values from -4 to 4
- second: float32 [1024, 512], P('shard'), may hold values from 0.01 to 0.5
- left_gram: float32 [1024, 1024], P('shard'), may hold values from -3 to 60, as said below
- left_basis: float32 [1024, 1024], P('shard'), may hold values from -0.1 to 1.1, as said below
- right_gram: float32 [512, 512], P('shard'), may hold values from -3 to 60, as said below
- right_basis: float32 [512, 512], P('shard'), may hold values from -0.1 to 1.1, as said below
Outputs:
- weight_new: float32 [1024, 512], P('shard')
- moment_new: float32 [1024, 512], P('shard')
- second_new: float32 [1024, 512], P('shard')
- left_new: float32 [1024, 1024], P('shard')
- left_basis_new: float32 [1024, 1024], P('shard')
- right_new: float32 [512, 512], P('shard')
- right_basis_new: float32 [512, 512], P('shard')
Inputs may be any that keep to these rules, and one draw needn't show every extreme that they name: `left_gram`: symmetric positive definite. `right_gram`: symmetric positive definite. `left_basis`: square and of full rank. `right_basis`: square and of full rank.
All inputs are finite; a program needn't handle non-finite values.
Results may differ from a plain program's by a relative error of at most 0.0015.
The roundings to bfloat16 on the way count: a program that leaves them out, or rounds other values in their place, can miss the bound.
Values may be sent and summed in bfloat16 or wider, within the bound.
No kernel may reach another device: no remote copies, remote signals or barrier semaphores. Data moves between devices by JAX's collectives and lax.ppermute only.
A program may use at most 64 MiB of HBM per device.

v0:
```python
import jax
import jax.numpy as jnp
from jax import lax
from jax.sharding import PartitionSpec as P

NS_ITERS = 2
BETA_ONE = 0.9
BETA_TWO = 0.95
GRAM_DECAY = 0.95
ADAM_EPS = 1e-08
NORM_EPS = 1e-06
STEP_SIZE = 0.02
START_SCALE = 0.75
PRECISE = lax.Precision.HIGHEST


def inner_rows(former, latter):
    return lax.dot_general(
        former, latter, (((0,), (0,)), ((), ())), preferred_element_type=jnp.float32
    )


def outer_rows(former, latter):
    return lax.dot_general(
        former, latter, (((1,), (1,)), ((), ())), preferred_element_type=jnp.float32
    )


def start_rows(power_rows, column_sums):
    scaled = START_SCALE * power_rows / jnp.sqrt(column_sums + NORM_EPS)
    return lax.optimization_barrier(scaled.astype(jnp.bfloat16))


def left_sweep(current):
    segment = lax.all_gather(current, "shard", axis=0, tiled=True)
    square = outer_rows(current, segment).astype(jnp.bfloat16)
    running = jnp.dot(square, segment, preferred_element_type=jnp.float32)
    return 1.5 * current.astype(jnp.float32) - 0.5 * running


def right_sweep(current):
    segment = lax.all_gather(current, "shard", axis=0, tiled=True)
    square = outer_rows(current, segment).astype(jnp.bfloat16)
    running = jnp.dot(square, segment, preferred_element_type=jnp.float32)
    return 1.5 * current.astype(jnp.float32) - 0.5 * running


def local(gradients, weight, moment, second, left_gram, left_basis, right_gram, right_basis):
    local_rows = weight.shape[0]
    right_rows = right_gram.shape[0]
    row_first = lax.axis_index("shard") * local_rows
    right_first = lax.axis_index("shard") * right_rows
    gradient = lax.psum(gradients[0], "grp") / lax.axis_size("grp")
    moment_new = BETA_ONE * moment + (1.0 - BETA_ONE) * gradient
    grad_half = gradient.astype(jnp.bfloat16)
    moment_half = moment_new.astype(jnp.bfloat16)
    left_half = left_basis.astype(jnp.bfloat16)
    right_whole = lax.all_gather(right_basis.astype(jnp.bfloat16), "shard", axis=0, tiled=True)
    right_wide = lax.optimization_barrier(right_whole).astype(jnp.float32)
    basis_part = lax.all_gather(left_half, "shard", axis=0, tiled=True)
    grad_part = lax.all_gather(grad_half, "shard", axis=0, tiled=True)
    basis_columns = lax.dynamic_slice_in_dim(basis_part, row_first, local_rows, 1)
    turned = inner_rows(basis_columns, grad_part)
    gram_block = GRAM_DECAY * left_gram + (1.0 - GRAM_DECAY) * outer_rows(grad_half, grad_part)
    power_rows = jnp.dot(gram_block, basis_part.astype(jnp.float32), precision=PRECISE)
    grad_columns = lax.dynamic_slice_in_dim(grad_part, right_first, right_rows, 1)
    right_terms = inner_rows(grad_columns, grad_part)
    core_state, basis_columns = ((turned, gram_block, power_rows, right_terms), basis_columns)
    core_state, turned_moment = (
        core_state,
        inner_rows(basis_columns, lax.all_gather(moment_half, "shard", axis=0, tiled=True)),
    )
    turned_grad, left_new, left_power, right_terms = core_state
    right_new = GRAM_DECAY * right_gram + (1.0 - GRAM_DECAY) * right_terms
    rotated_grad = jnp.dot(
        turned_grad.astype(jnp.bfloat16), right_whole, preferred_element_type=jnp.float32
    )
    rotated_moment = jnp.dot(
        turned_moment.astype(jnp.bfloat16), right_whole, preferred_element_type=jnp.float32
    )
    second_new = BETA_TWO * second + (1.0 - BETA_TWO) * rotated_grad * rotated_grad
    direction = (rotated_moment / (jnp.sqrt(second_new) + ADAM_EPS)).astype(jnp.bfloat16)
    returned = outer_rows(direction, right_whole).astype(jnp.bfloat16)
    update = jnp.dot(
        left_half,
        lax.all_gather(returned, "shard", axis=0, tiled=True),
        preferred_element_type=jnp.float32,
    )
    weight_new = weight - STEP_SIZE * update
    right_power = jnp.dot(right_new, right_wide, precision=PRECISE)
    left_sums, right_sums = lax.psum(
        (jnp.sum(left_power * left_power, axis=0), jnp.sum(right_power * right_power, axis=0)),
        "shard",
    )
    right_current = start_rows(right_power, right_sums)
    right_result = right_power
    for sweep in range(NS_ITERS):
        right_result = right_sweep(right_current)
        right_current = lax.optimization_barrier(right_result.astype(jnp.bfloat16))
    left_current = start_rows(left_power, left_sums)
    left_result = left_power
    for sweep in range(NS_ITERS):
        left_result = left_sweep(left_current)
        left_current = lax.optimization_barrier(left_result.astype(jnp.bfloat16))
    return (weight_new, moment_new, second_new, left_new, left_result, right_new, right_result)


def solution(mesh):
    return jax.shard_map(
        local,
        mesh=mesh,
        in_specs=(
            P("grp", "shard", None),
            P("shard", None),
            P("shard", None),
            P("shard", None),
            P("shard", None),
            P("shard", None),
            P("shard", None),
            P("shard", None),
        ),
        out_specs=(
            P("shard", None),
            P("shard", None),
            P("shard", None),
            P("shard", None),
            P("shard", None),
            P("shard", None),
            P("shard", None),
        ),
        check_vma=False,
    )
```

profile of v0, /device:TPU:2, one launch (start us, length us, event | category | flops | bytes accessed | tf_op | source)
XLA Modules:
  0.0 1857.0 jit_solution(10023106520451230898)
XLA Ops:
  7.2 36.2 %psum.21 = f32[16,512]{1,0:T(8,128)S(1)} all-reduce(f32[16,512]{1,0:T(8,128)} %bitcast.32), channel_id=1, replica_groups=mesh['grp'=8,'shard'=64] {'grp'}, use_global_device_ids=true, to_apply=%region_0.0 | all-reduce | flops 8192 | bytes 65536 | tf_op jit(solution)/shard_map/psum | solution.py:53
  43.4 1.4 fusion.29
  44.9 1.5 convert_element_type.62
  46.4 0.7 all-gather.9.cloned.1.call-update
  47.1 0.7 convert_element_type.65
  47.9 154.5 %all_gather.29 = bf16[512,512]{1,0:T(8,128)(2,1)S(1)} all-gather(bf16[8,512]{1,0:T(8,128)(2,1)S(1)} %convert_element_type.65), channel_id=1, replica_groups=mesh['grp'=8,'shard'=64] {'shard'}, dimensions={0}, use_global_device_ids=true | all-gather | bytes 532480 | tf_op jit(solution)/shard_map/all_gather | solution.py:58
  202.3 138.1 %all-gather.11.cloned.1.call-done = bf16[1024,512]{1,0:T(8,128)(2,1)} async-done(((bf16[16,512]{1,0:T(8,128)(2,1)}), bf16[1024,512]{1,0:T(8,128)(2,1)}) %all-gather.11.cloned.1.call-update) | async-done | bytes 1048592 | tf_op jit(solution)/shard_map/all_gather | solution.py:61
  340.4 1.7 fusion.8
  342.4 1.6 fusion.2
  344.1 298.7 %all-gather.7.cloned.1.call-done = bf16[1024,1024]{1,0:T(8,128)(2,1)} async-done(((bf16[16,1024]{1,0:T(8,128)(2,1)}), bf16[1024,1024]{1,0:T(8,128)(2,1)}) %all-gather.7.cloned.1.call-update) | async-done | bytes 2097168 | tf_op jit(solution)/shard_map/all_gather | solution.py:60
  642.8 2.5 multiply_reduce_fusion
  645.4 156.0 %all-reduce = (f32[1024]{0:T(1024)S(1)}, f32[512]{0:T(512)S(1)}) all-reduce(f32[1024]{0:T(1024)S(1)} %get-tuple-element.12, f32[512]{0:T(512)S(1)} %get-tuple-element.14), channel_id=1, replica_groups=mesh['grp'=8,'shard'=64] {'shard'}, use_global_device_ids=true, to_apply=%region_2.0 | all-reduce | flops 1536 | bytes 12288 | tf_op jit(solution)/shard_map/psum | solution.py:91
  802.1 140.5 %all-gather.9.cloned.1.call-done = bf16[1024,512]{1,0:T(8,128)(2,1)} async-done(((bf16[16,512]{1,0:T(8,128)(2,1)}), bf16[1024,512]{1,0:T(8,128)(2,1)}) %all-gather.9.cloned.1.call-update) | async-done | bytes 1048592 | tf_op jit(solution)/shard_map/all_gather | solution.py:71
  942.6 1.7 convolution_convert_fusion.3
  944.3 1.5 fusion.18
  945.8 1.0 convolution_convert_fusion.4
  946.8 298.1 %all-gather.15.cloned.1.call-done = bf16[1024,1024]{1,0:T(8,128)(2,1)} async-done(((bf16[16,1024]{1,0:T(8,128)(2,1)}), bf16[1024,1024]{1,0:T(8,128)(2,1)}) %all-gather.15.cloned.1.call-update) | async-done | bytes 2097168 | tf_op jit(solution)/shard_map/all_gather | solution.py:35
  1244.9 3.8 fusion.3
  1248.8 154.3 %all_gather.34 = bf16[512,512]{1,0:T(8,128)(2,1)S(1)} all-gather(bf16[8,512]{1,0:T(8,128)(2,1)S(1)} %divide_convert_fusion.1), channel_id=1, replica_groups=mesh['grp'=8,'shard'=64] {'shard'}, dimensions={0}, use_global_device_ids=true | all-gather | bytes 532480 | tf_op jit(solution)/shard_map/all_gather | solution.py:42
  1403.5 157.4 %all_gather.35 = bf16[512,512]{1,0:T(8,128)(2,1)S(1)} all-gather(bf16[8,512]{1,0:T(8,128)(2,1)S(1)} %fusion.11), channel_id=1, replica_groups=mesh['grp'=8,'shard'=64] {'shard'}, dimensions={0}, use_global_device_ids=true | all-gather | bytes 532480 | tf_op jit(solution)/shard_map/all_gather | solution.py:42
  1560.9 1.0 fusion.9
  1561.9 2.1 fusion.5
  1564.0 282.3 %all-gather.17.cloned.1.call-done = bf16[1024,1024]{1,0:T(8,128)(2,1)} async-done(((bf16[16,1024]{1,0:T(8,128)(2,1)}), bf16[1024,1024]{1,0:T(8,128)(2,1)}) %all-gather.17.cloned.1.call-update) | async-done | bytes 2097168 | tf_op jit(solution)/shard_map/all_gather | solution.py:35
  1846.3 3.8 fusion
  (40 shorter events, 1.8 us)
Async XLA Ops:
  7.2 335.3 %copy-start.8 = (f32[16,1024]{1,0:T(8,128)S(1)}, f32[16,1024]{1,0:T(8,128)}, u32[]{:S(2)}) copy-start(f32[16,1024]{1,0:T(8,128)} %param.12) | copy-start | bytes 196612
  7.2 333.2 %all-gather.11.cloned.1.call-start = ((), (), s32[]{:S(2)}) async-start(), calls=%async_computation.2 | async-start | bytes 1064960 | tf_op jit(solution)/shard_map/all_gather | solution.py:61
  44.8 297.6 %copy-start.5 = (bf16[16,512]{1,0:T(8,128)(2,1)S(1)}, bf16[16,512]{1,0:T(8,128)(2,1)}, u32[]{:S(2)}) copy-start(bf16[16,512]{1,0:T(8,128)(2,1)} %get-tuple-element.11) | copy-start | bytes 49156
  44.8 598.0 %all-gather.7.cloned.1.call-start = ((), (), s32[]{:S(2)}) async-start(), calls=%async_computation | async-start | bytes 2129920 | tf_op jit(solution)/shard_map/all_gather | solution.py:60
  46.4 896.2 %all-gather.9.cloned.1.call-start = ((), (), s32[]{:S(2)}) async-start(), calls=%async_computation.1 | async-start | bytes 1064960 | tf_op jit(solution)/shard_map/all_gather | solution.py:71
  47.1 1197.8 %all-gather.15.cloned.1.call-start = ((), (), s32[]{:S(2)}) async-start(), calls=%async_computation.4 | async-start | bytes 2129920 | tf_op jit(solution)/shard_map/all_gather | solution.py:35
  342.1 602.2 %copy-start.7 = (f32[8,512]{1,0:T(8,128)}, f32[8,512]{1,0:T(8,128)S(1)}, u32[]{:S(2)}) copy-start(f32[8,512]{1,0:T(8,128)S(1)} %fusion.8) | copy-start | bytes 49156
  344.0 601.7 %copy-start.4 = (f32[16,1024]{1,0:T(8,128)}, f32[16,1024]{1,0:T(8,128)S(1)}, u32[]{:S(2)}) copy-start(f32[16,1024]{1,0:T(8,128)S(1)} %fusion.2) | copy-start | bytes 196612
  344.0 600.2 %copy-start = (bf16[1024,512]{1,0:T(8,128)(2,1)S(1)}, bf16[1024,512]{1,0:T(8,128)(2,1)}, u32[]{:S(2)}) copy-start(bf16[1024,512]{1,0:T(8,128)(2,1)} %all-gather.11.cloned.1.call-done) | copy-start | bytes 3145732
  344.1 600.2 %copy-start.9 = (f32[16,512]{1,0:T(8,128)S(1)}, f32[16,512]{1,0:T(8,128)}, u32[]{:S(2)}) copy-start(f32[16,512]{1,0:T(8,128)} %param.11) | copy-start | bytes 98308
  802.0 759.9 %all-gather.13.cloned.1.call-start = ((), (), s32[]{:S(2)}) async-start(), calls=%async_computation.3 | async-start | bytes 1064960 | tf_op jit(solution)/shard_map/all_gather | solution.py:86
  802.0 442.9 %copy-start.2 = (bf16[16,1024]{1,0:T(8,128)(2,1)S(1)}, bf16[16,1024]{1,0:T(8,128)(2,1)}, u32[]{:S(2)}) copy-start(bf16[16,1024]{1,0:T(8,128)(2,1)} %divide_convert_fusion) | copy-start | bytes 98308
  945.8 303.0 %copy-start.6 = (f32[16,512]{1,0:T(8,128)}, f32[16,512]{1,0:T(8,128)S(1)}, u32[]{:S(2)}) copy-start(f32[16,512]{1,0:T(8,128)S(1)} %fusion.18) | copy-start | bytes 98308
  946.8 899.6 %all-gather.17.cloned.1.call-start = ((), (), s32[]{:S(2)}) async-start(), calls=%async_computation.5 | async-start | bytes 2129920 | tf_op jit(solution)/shard_map/all_gather | solution.py:35
  1248.7 313.2 %copy-start.3 = (bf16[16,1024]{1,0:T(8,128)(2,1)S(1)}, bf16[16,1024]{1,0:T(8,128)(2,1)}, u32[]{:S(2)}) copy-start(bf16[16,1024]{1,0:T(8,128)(2,1)} %convert_element_type.62) | copy-start | bytes 98308
  1248.7 313.2 %copy-start.10 = (f32[16,512]{1,0:T(8,128)S(1)}, f32[16,512]{1,0:T(8,128)}, u32[]{:S(2)}) copy-start(f32[16,512]{1,0:T(8,128)} %param.9) | copy-start | bytes 98308
  1248.8 597.6 %copy-start.1 = (bf16[16,1024]{1,0:T(8,128)(2,1)S(1)}, bf16[16,1024]{1,0:T(8,128)(2,1)}, u32[]{:S(2)}) copy-start(bf16[16,1024]{1,0:T(8,128)(2,1)} %fusion.3) | copy-start | bytes 98308
Sparse Core Ops, SparseCore 0:
  44.9 295.3 all-gather.10
  343.0 299.7 all-gather.6
  645.5 297.0 all-gather.8
  945.1 299.8 all-gather.14
  1246.9 297.0 all-gather.12
  1546.5 299.7 all-gather.16
where the time goes:
time: 1860 us
  waiting for transfers between devices  1160 us (62%)
  blocking collectives  658 us (35%)
  matrix products  21.4 us (1%)
    all_gather x2, waiting for transfers between devices, left_sweep(): segment = lax.all_gather(current, 'shard', axis=0, tiled=True)  580 us
    all_gather x2, blocking collectives, right_sweep(): segment = lax.all_gather(current, 'shard', axis=0, tiled=True)  312 us
    all_gather x1, waiting for transfers between devices, local(): basis_part = lax.all_gather(left_half, 'shard', axis=0, tiled=True)  299 us
    psum x1, blocking collectives, local(): lax.psum((jnp.sum(left_power * left_power, axis=0), jnp.sum(right_power *...  156 us
    all_gather x1, blocking collectives, local(): lax.all_gather(right_basis.astype(jnp.bfloat16), 'shard', axis=0, tiled=T...  154 us
    all_gather x1, waiting for transfers between devices, local(): lax.all_gather(moment_half, 'shard', axis=0, tiled=True)  141 us
    all_gather x1, waiting for transfers between devices, local(): grad_part = lax.all_gather(grad_half, 'shard', axis=0, tiled=True)  138 us
  transfers between devices with their start and end apart: 6, of which 5 were waited for; matrix products, arithmetic and copies ran while one was open for 1% of the time, Pallas kernels for 0%

commit v1 on v0

--- a/solution.py
+++ b/solution.py
@@ -57,7 +57,9 @@
     left_half = left_basis.astype(jnp.bfloat16)
     right_whole = lax.all_gather(right_basis.astype(jnp.bfloat16), "shard", axis=0, tiled=True)
     right_wide = lax.optimization_barrier(right_whole).astype(jnp.float32)
-    basis_part = lax.all_gather(left_half, "shard", axis=0, tiled=True)
+    basis_part = jnp.concatenate(
+        lax.all_to_all(jnp.stack([left_half] * lax.axis_size("shard")), "shard", 0, 0), axis=0
+    )
     grad_part = lax.all_gather(grad_half, "shard", axis=0, tiled=True)
     basis_columns = lax.dynamic_slice_in_dim(basis_part, row_first, local_rows, 1)
     turned = inner_rows(basis_columns, grad_part)

time: 1860 us -> 1570 us (0.84)
  waiting for transfers between devices: 1160 us -> 859 us
    all_gather x1 -> x0, waiting for transfers between devices: 299 us -> none  [local(): basis_part = lax.all_gather(left_half, 'shard', axis=0, tiled=True)]
  transfers between devices with their start and end apart: 6 -> 6, of which waited for: 5 -> 4; matrix products, arithmetic and copies ran while one was open for 1% -> 1% of each run, Pallas kernels for 0% -> 0%
where the time goes in v1:
time: 1570 us
  waiting for transfers between devices  859 us (55%)
  blocking collectives  662 us (42%)
  matrix products  20 us (1%)
    all_gather x2, waiting for transfers between devices, left_sweep(): segment = lax.all_gather(current, 'shard', axis=0, tiled=True)  580 us
    all_gather x2, blocking collectives, right_sweep(): segment = lax.all_gather(current, 'shard', axis=0, tiled=True)  312 us
    all_gather x1, blocking collectives, local(): lax.all_gather(right_basis.astype(jnp.bfloat16), 'shard', axis=0, tiled=T...  159 us
    psum x1, blocking collectives, local(): lax.psum((jnp.sum(left_power * left_power, axis=0), jnp.sum(right_power *...  156 us
    all_gather x1, waiting for transfers between devices, local(): grad_part = lax.all_gather(grad_half, 'shard', axis=0, tiled=True)  140 us
    all_gather x1, waiting for transfers between devices, local(): lax.all_gather(moment_half, 'shard', axis=0, tiled=True)  138 us
    psum x1, blocking collectives, local(): gradient = lax.psum(gradients[0], 'grp') / lax.axis_size('grp')  35.3 us
  transfers between devices with their start and end apart: 6, of which 4 were waited for; matrix products, arithmetic and copies ran while one was open for 1% of the time, Pallas kernels for 0%

profile of v1, /device:TPU:2, one launch (start us, length us, event | category | flops | bytes accessed | tf_op | source)
XLA Modules:
  0.0 1571.8 jit_solution(4135359234645867324)
XLA Ops:
  7.2 0.8 convert_element_type.62
  8.0 1.6 stack.2
  9.6 12.6 all-to-all-start
  22.3 35.3 %psum.21 = f32[16,512]{1,0:T(8,128)S(1)} all-reduce(f32[16,512]{1,0:T(8,128)S(1)} %bitcast.36), channel_id=1, replica_groups=mesh['grp'=8,'shard'=64] {'grp'}, use_global_device_ids=true, to_apply=%region_0.0 | all-reduce | flops 8192 | bytes 65536 | tf_op jit(solution)/shard_map/psum | solution.py:53
  57.6 0.6 fusion.29
  58.3 0.7 all-gather.6.cloned.1.call-update
  59.1 159.1 %all_gather.25 = bf16[512,512]{1,0:T(8,128)(2,1)S(1)} all-gather(bf16[8,512]{1,0:T(8,128)(2,1)S(1)} %convert_element_type.65), channel_id=1, replica_groups=mesh['grp'=8,'shard'=64] {'shard'}, dimensions={0}, use_global_device_ids=true | all-gather | bytes 532480 | tf_op jit(solution)/shard_map/all_gather | solution.py:58
  218.2 139.8 %all-gather.8.cloned.1.call-done = bf16[1024,512]{1,0:T(8,128)(2,1)} async-done(((bf16[16,512]{1,0:T(8,128)(2,1)}), bf16[1024,512]{1,0:T(8,128)(2,1)}) %all-gather.8.cloned.1.call-update) | async-done | bytes 1048592 | tf_op jit(solution)/shard_map/all_gather | solution.py:63
  358.0 1.7 fusion.8
  360.1 1.6 fusion.2
  361.7 0.9 multiply_reduce_fusion
  362.7 155.8 %all-reduce = (f32[1024]{0:T(1024)S(1)}, f32[512]{0:T(512)S(1)}) all-reduce(f32[1024]{0:T(1024)S(1)} %get-tuple-element.12, f32[512]{0:T(512)S(1)} %get-tuple-element.14), channel_id=1, replica_groups=mesh['grp'=8,'shard'=64] {'shard'}, use_global_device_ids=true, to_apply=%region_2.0 | all-reduce | flops 1536 | bytes 12288 | tf_op jit(solution)/shard_map/psum | solution.py:93
  519.2 138.4 %all-gather.6.cloned.1.call-done = bf16[1024,512]{1,0:T(8,128)(2,1)} async-done(((bf16[16,512]{1,0:T(8,128)(2,1)}), bf16[1024,512]{1,0:T(8,128)(2,1)}) %all-gather.6.cloned.1.call-update) | async-done | bytes 1048592 | tf_op jit(solution)/shard_map/all_gather | solution.py:73
  657.6 1.6 convolution_convert_fusion.3
  659.2 1.8 fusion.18
  661.0 1.0 convolution_convert_fusion.4
  662.0 298.1 %all-gather.12.cloned.1.call-done = bf16[1024,1024]{1,0:T(8,128)(2,1)} async-done(((bf16[16,1024]{1,0:T(8,128)(2,1)}), bf16[1024,1024]{1,0:T(8,128)(2,1)}) %all-gather.12.cloned.1.call-update) | async-done | bytes 2097168 | tf_op jit(solution)/shard_map/all_gather | solution.py:35
  960.1 3.8 fusion.3
  964.0 154.4 %all_gather.30 = bf16[512,512]{1,0:T(8,128)(2,1)S(1)} all-gather(bf16[8,512]{1,0:T(8,128)(2,1)S(1)} %divide_convert_fusion.1), channel_id=1, replica_groups=mesh['grp'=8,'shard'=64] {'shard'}, dimensions={0}, use_global_device_ids=true | all-gather | bytes 532480 | tf_op jit(solution)/shard_map/all_gather | solution.py:42
  1118.7 157.3 %all_gather.31 = bf16[512,512]{1,0:T(8,128)(2,1)S(1)} all-gather(bf16[8,512]{1,0:T(8,128)(2,1)S(1)} %fusion.11), channel_id=1, replica_groups=mesh['grp'=8,'shard'=64] {'shard'}, dimensions={0}, use_global_device_ids=true | all-gather | bytes 532480 | tf_op jit(solution)/shard_map/all_gather | solution.py:42
  1276.0 1.0 fusion.9
  1277.0 2.1 fusion.5
  1279.1 282.4 %all-gather.14.cloned.1.call-done = bf16[1024,1024]{1,0:T(8,128)(2,1)} async-done(((bf16[16,1024]{1,0:T(8,128)(2,1)}), bf16[1024,1024]{1,0:T(8,128)(2,1)}) %all-gather.14.cloned.1.call-update) | async-done | bytes 2097168 | tf_op jit(solution)/shard_map/all_gather | solution.py:35
  1561.5 3.8 fusion
  (44 shorter events, 1.7 us)
Async XLA Ops:
  9.6 12.7 copy-start.9
  9.6 48.0 %copy-start.10 = (f32[16,512]{1,0:T(8,128)S(1)}, f32[16,512]{1,0:T(8,128)}, u32[]{:S(2)}) copy-start(f32[16,512]{1,0:T(8,128)} %param.10) | copy-start | bytes 98308
  9.6 49.5 %copy-start.12 = (f32[8,512]{1,0:T(8,128)S(1)}, f32[8,512]{1,0:T(8,128)}, u32[]{:S(2)}) copy-start(f32[8,512]{1,0:T(8,128)} %param.15) | copy-start | bytes 49156
  9.6 348.4 %copy-start.11 = (f32[8,512]{1,0:T(8,128)S(1)}, f32[8,512]{1,0:T(8,128)}, u32[]{:S(2)}) copy-start(f32[8,512]{1,0:T(8,128)} %param.14) | copy-start | bytes 49156
  9.6 352.1 %all-to-all-start = ((bf16[64,16,1024]{2,1,0:T(8,128)(2,1)}), bf16[64,16,1024]{2,1,0:T(8,128)(2,1)S(1)}, u32[]{:S(2)}, u32[]{:S(2)}) async-start(bf16[64,16,1024]{2,1,0:T(8,128)(2,1)} %stack.2), calls=%async_computation | async-start | bytes 4194304 | tf_op jit(solution)/shard_map/all_to_all | solution.py:61
  22.2 337.8 %copy-start.6 = (f32[16,1024]{1,0:T(8,128)S(1)}, f32[16,1024]{1,0:T(8,128)}, u32[]{:S(2)}) copy-start(f32[16,1024]{1,0:T(8,128)} %param.12) | copy-start | bytes 196612
  22.2 335.7 %all-gather.8.cloned.1.call-start = ((), (), s32[]{:S(2)}) async-start(), calls=%async_computation.2 | async-start | bytes 1064960 | tf_op jit(solution)/shard_map/all_gather | solution.py:63
  58.3 301.8 %copy-start.3 = (bf16[16,512]{1,0:T(8,128)(2,1)S(1)}, bf16[16,512]{1,0:T(8,128)(2,1)}, u32[]{:S(2)}) copy-start(bf16[16,512]{1,0:T(8,128)(2,1)} %get-tuple-element.11) | copy-start | bytes 49156
  58.3 599.3 %all-gather.6.cloned.1.call-start = ((), (), s32[]{:S(2)}) async-start(), calls=%async_computation.1 | async-start | bytes 1064960 | tf_op jit(solution)/shard_map/all_gather | solution.py:73
  59.0 901.1 %all-gather.12.cloned.1.call-start = ((), (), s32[]{:S(2)}) async-start(), calls=%async_computation.4 | async-start | bytes 2129920 | tf_op jit(solution)/shard_map/all_gather | solution.py:35
  359.7 299.5 %copy-start.5 = (f32[8,512]{1,0:T(8,128)}, f32[8,512]{1,0:T(8,128)S(1)}, u32[]{:S(2)}) copy-start(f32[8,512]{1,0:T(8,128)S(1)} %fusion.8) | copy-start | bytes 49156
  361.7 299.3 %copy-start.2 = (f32[16,1024]{1,0:T(8,128)}, f32[16,1024]{1,0:T(8,128)S(1)}, u32[]{:S(2)}) copy-start(f32[16,1024]{1,0:T(8,128)S(1)} %fusion.2) | copy-start | bytes 196612
  361.7 297.5 %copy-start.7 = (f32[16,512]{1,0:T(8,128)S(1)}, f32[16,512]{1,0:T(8,128)}, u32[]{:S(2)}) copy-start(f32[16,512]{1,0:T(8,128)} %param.11) | copy-start | bytes 98308
  519.1 757.9 %all-gather.10.cloned.1.call-start = ((), (), s32[]{:S(2)}) async-start(), calls=%async_computation.3 | async-start | bytes 1064960 | tf_op jit(solution)/shard_map/all_gather | solution.py:88
  519.2 440.9 %copy-start.1 = (bf16[16,1024]{1,0:T(8,128)(2,1)S(1)}, bf16[16,1024]{1,0:T(8,128)(2,1)}, u32[]{:S(2)}) copy-start(bf16[16,1024]{1,0:T(8,128)(2,1)} %divide_convert_fusion) | copy-start | bytes 98308
  661.0 302.9 %copy-start.4 = (f32[16,512]{1,0:T(8,128)}, f32[16,512]{1,0:T(8,128)S(1)}, u32[]{:S(2)}) copy-start(f32[16,512]{1,0:T(8,128)S(1)} %fusion.18) | copy-start | bytes 98308
  662.0 899.5 %all-gather.14.cloned.1.call-start = ((), (), s32[]{:S(2)}) async-start(), calls=%async_computation.5 | async-start | bytes 2129920 | tf_op jit(solution)/shard_map/all_gather | solution.py:35
  963.9 313.1 %copy-start.8 = (f32[16,512]{1,0:T(8,128)S(1)}, f32[16,512]{1,0:T(8,128)}, u32[]{:S(2)}) copy-start(f32[16,512]{1,0:T(8,128)} %param.9) | copy-start | bytes 98308
  963.9 597.5 %copy-start = (bf16[16,1024]{1,0:T(8,128)(2,1)S(1)}, bf16[16,1024]{1,0:T(8,128)(2,1)}, u32[]{:S(2)}) copy-start(bf16[16,1024]{1,0:T(8,128)(2,1)} %fusion.3) | copy-start | bytes 98308
Sparse Core Ops, SparseCore 0:
  58.4 299.5 all-gather.7
  360.6 296.9 all-gather.5
  660.2 299.8 all-gather.11
  962.0 297.1 all-gather.9
  1261.7 299.7 all-gather.13
